TPU v7x, 32 devices: a whole 2x2x4 slice. The times are simulated.
32 devices in a mesh: gx: 8 (over z, core), gy: 4 (over y, x).
Axes of the slice: x: 2, y: 2, z: 4, core: 2. Of those that a mesh axis runs over, the one named last changes fastest.
Arguments:
- tracers: bfloat16 [8, 64, 32, 256], P(None, 'gx', 'gy'), may hold values from -6 to 6
- velocity: float32 [2, 64, 32], P(None, 'gx', 'gy'), may hold values from -0.04 to 0.04
- inflow: int32 [4, 64, 32], P(None, 'gx', 'gy'), may hold values from 0 to 1, as said below
- leaf_solve: float32 [256, 256], replicated, may hold values from -0.375 to 0.375
- leaf_skeleton: float32 [256, 64], replicated, may hold values from -0.375 to 0.375
- leaf_lift: float32 [64, 256], replicated, may hold values from -0.75 to 0.75
- merge_first: float32 [128, 64], replicated, may hold values from -0.5 to 0.5
- merge_second: float32 [128, 128], replicated, may hold values from -0.5 to 0.5
- merge_rest: float32 [9, 256, 128], replicated, may hold values from -0.375 to 0.375
- parent_first: float32 [64, 128], replicated, may hold values from -0.75 to 0.75
- parent_second: float32 [128, 128], replicated, may hold values from -0.5 to 0.5
- parent_rest: float32 [9, 128, 256], replicated, may hold values from -0.5 to 0.5
- sibling_first: float32 [128, 128], replicated, may hold values from -0.125 to 0.125
- sibling_second: float32 [128, 128], replicated, may hold values from -0.125 to 0.125
- sibling_rest: float32 [9, 256, 256], replicated, may hold values from -0.09375 to 0.09375
- root_map: float32 [128, 128], replicated, may hold values from -0.5 to 0.5
Outputs:
- updated: bfloat16 [8, 64, 32, 256], P(None, 'gx', 'gy')
Inputs may be any that keep to these rules, and one draw needn't show every extreme that they name: inflow[0] of leaf (i, j) equals 1 minus inflow[1] of leaf (i - 1, j), and inflow[2] of leaf (i, j) equals 1 minus inflow[3] of leaf (i, j - 1); inflow[1] is 0 on the last leaves along the first dimension and inflow[3] on the last leaves along the second.
All inputs are finite; a program needn't handle non-finite values.
Results may differ from a plain program's by a relative error of at most 0.001.
Values may be sent and summed in bfloat16 or wider, within the bound.
A program may use at most 64 MiB of HBM per device.

v0:
```python
import jax
import jax.numpy as jnp
from jax import lax
from jax.sharding import PartitionSpec as P

NODE = 16


highest = lax.Precision.HIGHEST


def padded_2(cells, sides, width):
    for axis, dim in sides:
        count = lax.axis_size(axis)
        ends = count - 1
        head = lax.slice_in_dim(cells, 0, width, axis=dim)
        tail = lax.slice_in_dim(cells, cells.shape[dim] - width, cells.shape[dim], axis=dim)
        cells = jnp.concatenate(
            [
                lax.ppermute(tail, axis, [(i, (i + 1) % count) for i in range(ends)]),
                cells,
                lax.ppermute(head, axis, [((i + 1) % count, i) for i in range(ends)]),
            ],
            axis=dim,
        )
    return cells


def from_partner(array, axis, stride):
    return lax.ppermute(array, axis, [(i, i ^ 1 << stride) for i in range(lax.axis_size(axis))])


def product(left, right):
    return jnp.dot(left, right, precision=highest, preferred_element_type=jnp.float32)


def spectral_matrix(node_count):
    node_index = jnp.arange(node_count)
    points = -jnp.cos(jnp.pi * node_index.astype(jnp.float32) / (node_count - 1))
    end_weights = jnp.where((node_index == 0) | (node_index == node_count - 1), 2.0, 1.0)
    parity = jnp.where(node_index % 2 == 0, 1.0, -1.0)
    weights = (end_weights * parity).astype(jnp.float32)
    identity = jnp.eye(node_count, dtype=jnp.float32)
    offsets = points[:, None] - points[None, :] + identity
    matrix = weights[:, None] / weights[None, :] / offsets * (1.0 - identity)
    return matrix - jnp.diag(jnp.sum(matrix, axis=1))


def derivative_tables(node_count):
    spectral = spectral_matrix(node_count)
    identity = jnp.eye(node_count, dtype=jnp.float32)
    return jnp.concatenate([jnp.kron(spectral, identity).T, jnp.kron(identity, spectral).T], axis=1)


def side_table(node_count):
    node_index = jnp.arange(node_count * node_count)
    along_first = node_index // node_count
    along_second = node_index % node_count
    position = jnp.arange(node_count)[:, None]
    table_rows = [
        (along_first[None, :] == 0) & (along_second[None, :] == position),
        (along_first[None, :] == node_count - 1) & (along_second[None, :] == position),
        (along_second[None, :] == 0) & (along_first[None, :] == position),
        (along_second[None, :] == node_count - 1) & (along_first[None, :] == position),
    ]
    return jnp.concatenate(table_rows, axis=0).astype(jnp.float32)


def edge_values(tracer_field, node_count):
    node_grid = tracer_field.reshape(tracer_field.shape[:-1] + (node_count, node_count))
    return (
        node_grid[..., 0, :],
        node_grid[..., node_count - 1, :],
        node_grid[..., :, 0],
        node_grid[..., :, node_count - 1],
    )


def forcing_term(tracer_field, own_edges, neighbours, velocity, inflow):
    node_count = own_edges[0].shape[-1]
    square = node_count * node_count
    gradients = product(tracer_field, derivative_tables(node_count))
    advective = (
        velocity[0][None, :, :, None] * gradients[..., :square]
        + velocity[1][None, :, :, None] * gradients[..., square:]
    )
    penalty_terms = []
    for side_index in range(4):
        strength = inflow[side_index].astype(jnp.float32) * (
            node_count * jnp.abs(velocity[side_index // 2])
        )
        penalty_terms.append(
            strength[None, :, :, None] * (neighbours[side_index] - own_edges[side_index])
        )
    penalty = product(jnp.concatenate(penalty_terms, axis=-1), side_table(node_count))
    return tracer_field - advective + penalty


def level_operators(level, tables):
    if level == 0:
        return tables[0]
    if level == 1:
        return tables[1]
    return tuple((stacked[level - 2] for stacked in tables[2]))


def split_pairs(current, merge_axis):
    new_shape = (
        current.shape[:merge_axis]
        + (current.shape[merge_axis] // 2, 2)
        + current.shape[merge_axis + 1 :]
    )
    paired = current.reshape(new_shape)
    return (
        lax.index_in_dim(paired, 0, merge_axis + 1, False),
        lax.index_in_dim(paired, 1, merge_axis + 1, False),
    )


def join_pairs(former, latter, merge_axis):
    joined = jnp.stack([former, latter], axis=merge_axis + 1)
    new_shape = list(former.shape)
    new_shape[merge_axis] = new_shape[merge_axis] * 2
    return joined.reshape(tuple(new_shape))


def ascend(current, merge_plan, start_level, tables):
    levels = []
    for offset, merge_axis in enumerate(merge_plan):
        level = start_level + offset
        former, latter = split_pairs(current, merge_axis)
        levels.append((former, latter, merge_axis, level))
        current = product(
            jnp.concatenate([former, latter], axis=-1), level_operators(level, tables)[0]
        )
    return (current, levels)


def descend(boundary, levels, tables):
    for former, latter, merge_axis, level in reversed(levels):
        operators = level_operators(level, tables)
        joined_pair = product(boundary, operators[1]) + product(
            jnp.concatenate([former, latter], axis=-1), operators[2]
        )
        half_width = joined_pair.shape[-1] // 2
        boundary = join_pairs(
            joined_pair[..., :half_width], joined_pair[..., half_width:], merge_axis
        )
    return boundary


def local_plan(leaf_side):
    merge_plan = []
    block_span = leaf_side
    while block_span > 1:
        merge_plan = merge_plan + [1, 2]
        block_span = block_span // 2
    return merge_plan


def cross_plan(count_first, count_second):
    merge_plan = []
    while count_first * count_second > 1:
        if count_first >= count_second:
            merge_plan.append(1)
            count_first = count_first // 2
        else:
            merge_plan.append(2)
            count_second = count_second // 2
    return merge_plan


def local(
    tracers,
    velocity,
    inflow,
    leaf_solve,
    leaf_skeleton,
    leaf_lift,
    merge_first,
    merge_second,
    merge_rest,
    parent_first,
    parent_second,
    parent_rest,
    sibling_first,
    sibling_second,
    sibling_rest,
    root_map,
):
    tables = (
        (merge_first, parent_first, sibling_first),
        (merge_second, parent_second, sibling_second),
        (merge_rest, parent_rest, sibling_rest),
    )
    tracer_count, leaf_side = (tracers.shape[0], tracers.shape[1])
    tracer_field = tracers.astype(jnp.float32)
    own_edges = edge_values(tracer_field, NODE)
    padded = padded_2(tracers, (("gx", 1), ("gy", 2)), 1)
    node_grid = padded.reshape(padded.shape[:-1] + (NODE, NODE))
    neighbours = (
        node_grid[:, :leaf_side, 1 : leaf_side + 1, NODE - 1, :],
        node_grid[:, 2:, 1 : leaf_side + 1, 0, :],
        node_grid[:, 1 : leaf_side + 1, :leaf_side, :, NODE - 1],
        node_grid[:, 1 : leaf_side + 1, 2:, :, 0],
    )
    neighbours = tuple((edge_line.astype(jnp.float32) for edge_line in neighbours))
    forcing = forcing_term(tracer_field, own_edges, neighbours, velocity, inflow)
    skeleton = product(forcing, leaf_skeleton)
    block_plan = local_plan(leaf_side)
    block_root, local_levels = ascend(skeleton, block_plan, 0, tables)
    first_cross = len(block_plan)
    device_root = block_root[:, 0, 0]
    count_first, count_second = (lax.axis_size("gx"), lax.axis_size("gy"))
    merge_plan = cross_plan(count_first, count_second)
    current = device_root
    history = []
    bits_first, bits_second = (0, 0)
    for offset, merge_axis in enumerate(merge_plan):
        level = first_cross + offset
        if merge_axis == 1:
            partner = from_partner(current, "gx", bits_first)
            position = lax.axis_index("gx") // 2**bits_first % 2
            bits_first = bits_first + 1
        else:
            partner = from_partner(current, "gy", bits_second)
            position = lax.axis_index("gy") // 2**bits_second % 2
            bits_second = bits_second + 1
        is_latter = position == 1
        former = jnp.where(is_latter, partner, current)
        latter = jnp.where(is_latter, current, partner)
        history.append((former, latter, level, is_latter))
        current = product(
            jnp.concatenate([former, latter], axis=-1), level_operators(level, tables)[0]
        )
    boundary = product(current, root_map)
    for former, latter, level, is_latter in reversed(history):
        operators = level_operators(level, tables)
        joined_pair = product(boundary, operators[1]) + product(
            jnp.concatenate([former, latter], axis=-1), operators[2]
        )
        half_width = joined_pair.shape[-1] // 2
        boundary = jnp.where(is_latter, joined_pair[:, half_width:], joined_pair[:, :half_width])
    leaf_boundary = descend(boundary[:, None, None, :], local_levels, tables)
    updated = product(forcing, leaf_solve) + product(leaf_boundary, leaf_lift)
    return updated.astype(jnp.bfloat16)


def solution(mesh):
    in_specs = (
        P(None, "gx", "gy", None),
        P(None, "gx", "gy"),
        P(None, "gx", "gy"),
        P(),
        P(),
        P(),
        P(),
        P(),
        P(),
        P(),
        P(),
        P(),
        P(),
        P(),
        P(),
        P(),
    )
    out_specs = P(None, "gx", "gy", None)
    return jax.shard_map(local, mesh=mesh, in_specs=in_specs, out_specs=out_specs, check_vma=False)
```

profile of v0, /device:TPU:0, one launch (start us, length us, event | category | flops | bytes accessed | tf_op | source)
XLA Modules:
  0.0 109.0 jit_solution(2128812930580505567)
XLA Ops:
  0.0 0.8 fusion.166
  0.8 2.4 %collective-permute-start = (bf16[8,1,8,256]{3,2,1,0:T(8,128)(2,1)S(1)}, bf16[8,1,8,256]{3,2,1,0:T(8,128)(2,1)S(1)}, u32[]{:S(2)}, u32[]{:S(2)}) collective-permute-start(bf16[8,1,8,256]{3,2,1,0:T(8,128)(2,1)S(1)} %get-tuple-element.16), channel_id=1, source_target_pairs={{0,4},{4,8},{8,12},{12,16},{16,20},{20,24},{24,28},{1,5},{5,9},{9,... | collective-permute-start | bytes 98312 | tf_op jit(solution)/shard_map/ppermute | solution.py:20
  3.2 1.3 %collective-permute-start.1 = (bf16[8,1,8,256]{3,2,1,0:T(8,128)(2,1)S(1)}, bf16[8,1,8,256]{3,2,1,0:T(8,128)(2,1)S(1)}, u32[]{:S(2)}, u32[]{:S(2)}) collective-permute-start(bf16[8,1,8,256]{3,2,1,0:T(8,128)(2,1)S(1)} %get-tuple-element.15), channel_id=1, source_target_pairs={{4,0},{8,4},{12,8},{16,12},{20,16},{24,20},{28,24},{5,1},{9,5},{13... | collective-permute-start | bytes 98312 | tf_op jit(solution)/shard_map/ppermute | solution.py:22
  4.5 3.7 %reshape.384 = f32[8,8,8,16,16]{4,3,2,1,0:T(8,128)} reshape(bf16[8,8,8,256]{3,2,1,0:T(8,128)(2,1)} %param.16) | data formatting | bytes 786432 | tf_op jit(solution)/shard_map/reshape | solution.py:70
  8.2 3.6 %fusion.162 = (f32[8,8,8,1,16]{4,3,2,1,0:T(1,128)}, f32[8,8,8,1,16]{4,3,2,1,0:T(1,128)}) fusion(f32[8,8,8,16,16]{4,3,2,1,0:T(8,128)} %reshape.384), kind=kLoop, calls=%fused_computation.275 | loop fusion | bytes 131072 | tf_op jit(solution)/shard_map/slice | solution.py:72
  11.8 8.2 %fusion.163 = (f32[8,8,8,16,1]{4,3,2,1,0:T(8,128)}, f32[8,8,8,16,1]{4,3,2,1,0:T(8,128)}) fusion(f32[8,8,8,16,16]{4,3,2,1,0:T(8,128)} %reshape.384), kind=kLoop, calls=%fused_computation.276 | loop fusion | bytes 131072 | tf_op jit(solution)/shard_map/slice | solution.py:74
  20.1 0.6 slice_bitcast_fusion.21
  20.9 1.6 %broadcast_multiply_fusion.1 = (f32[16,16,16,16]{1,0,3,2:T(8,128)}, f32[16,16,16,16]{1,0,3,2:T(8,128)S(1)}) fusion(f32[16,16]{0,1:T(8,128)S(1)} %fusion.120, f32[16,16]{0,1:T(8,128)S(1)} %select_subtract_fusion), kind=kLoop, calls=%fused_computation.21 | loop fusion | flops 131072 | bytes 526336 | tf_op jit(solution)/shard_map/jit(kron)/mul | solution.py:52
  22.5 2.5 %mul.179 = f32[256,256]{0,1:T(8,128)S(1)} reshape(f32[16,16,16,16]{1,0,3,2:T(8,128)} %get-tuple-element.41) | data formatting | bytes 524288 | tf_op jit(solution)/shard_map/jit(kron)/mul | solution.py:52
  25.0 0.9 mul.183
  25.9 1.6 %convolution_bitcast_fusion = f32[8,8,8,512]{3,2,1,0:T(8,128)} fusion(bf16[8,8,8,256]{3,2,1,0:T(8,128)(2,1)S(1)} %copy-done.3, f32[256,256]{1,0:T(8,128)S(1)} %bitcast.324, f32[256,256]{1,0:T(8,128)S(1)} %bitcast.323), kind=kOutput, calls=%fused_computation.1 | convolution fusion | flops 805437440 | bytes 1835008 | tf_op jit(solution)/shard_map/dot_general | solution.py:34
  27.5 0.6 fusion.117
  28.3 4.2 %collective-permute-start.2 = (bf16[8,10,1,256]{3,2,1,0:T(2,128)(2,1)S(1)}, bf16[8,10,1,256]{3,2,1,0:T(2,128)(2,1)S(1)}, u32[]{:S(2)}, u32[]{:S(2)}) collective-permute-start(bf16[8,10,1,256]{3,2,1,0:T(2,128)(2,1)S(1)} %get-tuple-element.11), channel_id=1, source_target_pairs={{0,1},{1,2},{2,3},{4,5},{5,6},{6,7},{8,9},{9,10},{10,11},{12,13},{... | collective-permute-start | bytes 122888 | tf_op jit(solution)/shard_map/ppermute | solution.py:20
  32.5 1.3 %collective-permute-start.3 = (bf16[8,10,1,256]{3,2,1,0:T(2,128)(2,1)S(1)}, bf16[8,10,1,256]{3,2,1,0:T(2,128)(2,1)S(1)}, u32[]{:S(2)}, u32[]{:S(2)}) collective-permute-start(bf16[8,10,1,256]{3,2,1,0:T(2,128)(2,1)S(1)} %get-tuple-element.12), channel_id=1, source_target_pairs={{1,0},{2,1},{3,2},{5,4},{6,5},{7,6},{9,8},{10,9},{11,10},{13,12},{... | collective-permute-start | bytes 122888 | tf_op jit(solution)/shard_map/ppermute | solution.py:22
  33.8 0.6 fusion.115
  34.4 5.4 %copy.115 = f32[8,8,8,16,1]{3,2,1,0,4:T(8,128)} copy(f32[8,8,8,16,1]{4,3,2,1,0:T(8,128)} %get-tuple-element.7) | data formatting | bytes 65536
  39.8 0.4 pad_maximum_fusion
  40.2 1.0 copy.72
  41.2 3.6 %reshape.383 = bf16[8,10,10,16,16]{4,3,0,2,1:T(8,128)(2,1)S(1)} reshape(bf16[8,10,10,256]{3,0,2,1:T(8,128)(2,1)} %copy.72) | data formatting | bytes 819200 | tf_op jit(solution)/shard_map/reshape | solution.py:200
  44.8 1.3 %fusion.164 = (bf16[8,8,8,1,16]{4,3,0,2,1:T(2,128)(2,1)}, bf16[8,8,8,1,16]{4,3,0,2,1:T(2,128)(2,1)}) fusion(bf16[8,10,10,16,16]{4,3,0,2,1:T(8,128)(2,1)S(1)} %reshape.383), kind=kLoop, calls=%fused_computation.277 | loop fusion | bytes 65536 | tf_op jit(solution)/shard_map/slice | solution.py:202
  46.2 2.1 %slice.336 = bf16[8,8,8,16,1]{4,3,0,2,1:T(8,128)(2,1)} slice(bf16[8,10,10,16,16]{4,3,0,2,1:T(8,128)(2,1)S(1)} %reshape.383), slice={[0:8], [1:9], [0:8], [0:16], [15:16]} | slice | bytes 32768 | tf_op jit(solution)/shard_map/slice | solution.py:204
  48.2 0.9 copy-done.1
  49.1 2.7 %copy_subtract_fusion = f32[8,8,8,16,1]{4,3,0,2,1:T(8,128)} fusion(f32[8,8,8,16,1]{4,3,2,1,0:T(8,128)S(1)} %copy-done.1, bf16[8,10,10,16,16]{4,3,0,2,1:T(8,128)(2,1)S(1)} %reshape.383), kind=kLoop, calls=%fused_computation | loop fusion | flops 16384 | bytes 81920 | tf_op jit(solution)/shard_map/sub | solution.py:93
  51.8 4.9 %copy.80 = f32[8,8,8,16,1]{3,2,1,0,4:T(8,128)S(1)} copy(f32[8,8,8,16,1]{4,3,0,2,1:T(8,128)} %copy_subtract_fusion) | data formatting | bytes 65536 | tf_op jit(solution)/shard_map/sub | solution.py:93
  56.7 3.5 %copy.114 = bf16[8,8,8,16,1]{3,2,1,0,4:T(8,128)(2,1)S(1)} copy(bf16[8,8,8,16,1]{4,3,0,2,1:T(8,128)(2,1)S(1)} %copy-done.2) | data formatting | bytes 32768
  60.4 1.4 %bitcast_multiply_fusion.2 = (f32[8,8,8,16]{3,2,1,0:T(8,128)S(1)}, f32[8,8,8,16]{3,2,1,0:T(8,128)S(1)}) fusion(f32[8,8,8,1,16]{4,2,3,1,0:T(8,128)} %bitcast.316, bf16[8,8,8,1,16]{4,3,0,2,1:T(2,128)(2,1)} %get-tuple-element.10, f32[8,8]{1,0:T(8,128)S(1)} %get-tuple-element.34, f32[8,8,8,1,16]{4,2,3,1,0:T(8,128)S(1)} %bitcast.315, ...), kind=kLoop, calls=%fused_computation.52 | loop fusion | flops 49152 | bytes 164352 | tf_op jit(solution)/shard_map/mul | solution.py:93
  61.9 0.5 convolution_add_fusion
  62.5 0.6 fusion.101
  63.1 0.3 fusion.109
  63.6 0.3 fusion.99
  63.9 0.6 fusion.168
  64.5 1.1 %fusion.39 = f32[8,2,2,2,128]{4,0,3,2,1:T(8,128)S(1)} fusion(f32[9,256,128]{2,1,0:T(8,128)} %param.24, f32[8,2,2,2,128]{4,0,3,2,1:T(8,128)S(1)} %bitcast.329, f32[8,2,2,2,128]{4,0,3,2,1:T(8,128)S(1)} %bitcast.328), kind=kOutput, calls=%fused_computation.73 | convolution fusion | flops 25182208 | bytes 229376 | tf_op jit(solution)/shard_map/dot_general | solution.py:34
  65.6 0.6 copy-done.10
  66.2 1.1 %convolution_bitcast_fusion.1 = f32[8,1,2,2,128]{4,0,3,2,1:T(8,128)S(1)} fusion(f32[9,256,128]{2,1,0:T(8,128)} %param.24, f32[8,2,2,128]{3,0,2,1:T(8,128)S(1)} %get-tuple-element.32, f32[8,2,2,128]{3,0,2,1:T(8,128)S(1)} %get-tuple-element.31), kind=kOutput, calls=%fused_computation.11 | convolution fusion | flops 12591104 | bytes 180224 | tf_op jit(solution)/shard_map/dot_general | solution.py:34
  67.3 0.6 copy-done.12
  67.9 1.1 convolution_bitcast_fusion.2
  69.0 0.6 copy-done.23
  69.6 1.7 %fusion.65 = f32[8,128]{1,0:T(8,128)} fusion(f32[9,256,128]{2,1,0:T(8,128)} %param.24, f32[8,1,1,128]{3,0,2,1:T(8,128)S(1)} %get-tuple-element.56, f32[8,1,1,128]{3,0,2,1:T(8,128)S(1)} %get-tuple-element.55), kind=kOutput, calls=%fused_computation.99 | convolution fusion | flops 3147776 | bytes 143360 | tf_op jit(solution)/shard_map/dot_general | solution.py:34
  71.3 2.2 %collective-permute-start.4 = (f32[8,128]{1,0:T(8,128)}, f32[8,128]{1,0:T(8,128)}, u32[]{:S(2)}, u32[]{:S(2)}) collective-permute-start(f32[8,128]{1,0:T(8,128)} %fusion.65), channel_id=1, source_target_pairs={{0,4},{4,0},{8,12},{12,8},{16,20},{20,16},{24,28},{28,24},{1,5},{5... | collective-permute-start | bytes 12296 | tf_op jit(solution)/shard_map/ppermute | solution.py:30
  73.5 1.2 %collective-permute-done.4 = f32[8,128]{1,0:T(8,128)} collective-permute-done((f32[8,128]{1,0:T(8,128)}, f32[8,128]{1,0:T(8,128)}, u32[]{:S(2)}, u32[]{:S(2)}) %collective-permute-start.4) | collective-permute-done | bytes 4128 | tf_op jit(solution)/shard_map/ppermute | solution.py:30
  74.7 0.7 broadcast_select_fusion.9
  75.4 0.6 copy-done.27
  75.9 1.7 %fusion.63 = f32[8,128]{1,0:T(8,128)} fusion(f32[9,256,128]{2,1,0:T(8,128)} %param.24, f32[8,128]{1,0:T(8,128)S(1)} %get-tuple-element.54, f32[8,128]{1,0:T(8,128)S(1)} %get-tuple-element.53), kind=kOutput, calls=%fused_computation.97 | convolution fusion | flops 3147776 | bytes 143360 | tf_op jit(solution)/shard_map/dot_general | solution.py:34
  77.6 2.2 %collective-permute-start.5 = (f32[8,128]{1,0:T(8,128)}, f32[8,128]{1,0:T(8,128)}, u32[]{:S(2)}, u32[]{:S(2)}) collective-permute-start(f32[8,128]{1,0:T(8,128)} %fusion.63), channel_id=1, source_target_pairs={{0,8},{4,12},{8,0},{12,4},{16,24},{20,28},{24,16},{28,20},{1,9},{5... | collective-permute-start | bytes 12296 | tf_op jit(solution)/shard_map/ppermute | solution.py:30
  79.9 1.9 %collective-permute-done.5 = f32[8,128]{1,0:T(8,128)} collective-permute-done((f32[8,128]{1,0:T(8,128)}, f32[8,128]{1,0:T(8,128)}, u32[]{:S(2)}, u32[]{:S(2)}) %collective-permute-start.5) | collective-permute-done | bytes 4128 | tf_op jit(solution)/shard_map/ppermute | solution.py:30
  81.8 0.7 broadcast_select_fusion.7
  82.4 0.6 copy-done.31
  83.0 1.7 %fusion.61 = f32[8,128]{1,0:T(8,128)} fusion(f32[9,256,128]{2,1,0:T(8,128)} %param.24, f32[8,128]{1,0:T(8,128)S(1)} %get-tuple-element.52, f32[8,128]{1,0:T(8,128)S(1)} %get-tuple-element.51), kind=kOutput, calls=%fused_computation.95 | convolution fusion | flops 3147776 | bytes 143360 | tf_op jit(solution)/shard_map/dot_general | solution.py:34
  84.7 2.6 %collective-permute-start.6 = (f32[8,128]{1,0:T(8,128)}, f32[8,128]{1,0:T(8,128)}, u32[]{:S(2)}, u32[]{:S(2)}) collective-permute-start(f32[8,128]{1,0:T(8,128)} %fusion.61), channel_id=1, source_target_pairs={{0,1},{1,0},{2,3},{3,2},{4,5},{5,4},{6,7},{7,6},{8,9},{9,8},{10,11... | collective-permute-start | bytes 12296 | tf_op jit(solution)/shard_map/ppermute | solution.py:30
  87.4 1.9 %collective-permute-done.6 = f32[8,128]{1,0:T(8,128)} collective-permute-done((f32[8,128]{1,0:T(8,128)}, f32[8,128]{1,0:T(8,128)}, u32[]{:S(2)}, u32[]{:S(2)}) %collective-permute-start.6) | collective-permute-done | bytes 4128 | tf_op jit(solution)/shard_map/ppermute | solution.py:30
  89.3 0.7 broadcast_select_fusion.5
  89.9 1.1 fusion.59
  91.0 3.1 %collective-permute-start.7 = (f32[8,128]{1,0:T(8,128)S(1)}, f32[8,128]{1,0:T(8,128)S(1)}, u32[]{:S(2)}, u32[]{:S(2)}) collective-permute-start(f32[8,128]{1,0:T(8,128)S(1)} %fusion.59), channel_id=1, source_target_pairs={{0,16},{4,20},{8,24},{12,28},{16,0},{20,4},{24,8},{28,12},{1,17},{... | collective-permute-start | bytes 12296 | tf_op jit(solution)/shard_map/ppermute | solution.py:30
  94.1 0.6 fusion.17
  94.8 1.0 collective-permute-done.7
  95.7 1.1 fusion.57
  96.8 3.0 %collective-permute-start.8 = (f32[8,128]{1,0:T(8,128)S(1)}, f32[8,128]{1,0:T(8,128)S(1)}, u32[]{:S(2)}, u32[]{:S(2)}) collective-permute-start(f32[8,128]{1,0:T(8,128)S(1)} %fusion.57), channel_id=1, source_target_pairs={{0,2},{1,3},{2,0},{3,1},{4,6},{5,7},{6,4},{7,5},{8,10},{9,11},{10,... | collective-permute-start | bytes 12296 | tf_op jit(solution)/shard_map/ppermute | solution.py:30
  99.8 1.0 fusion.14
  100.9 0.6 collective-permute-done.8
  101.4 1.1 fusion.55
  106.6 0.3 convolution_add_fusion.3
  107.0 0.2 fusion.68
  107.2 0.3 convolution_add_fusion.2
  107.7 1.3 %fusion = bf16[8,8,8,256]{3,2,1,0:T(8,128)(2,1)} fusion(f32[8,8,8,256]{3,2,1,0:T(8,128)S(1)} %fusion.17, f32[8,8,8,64]{3,2,1,0:T(8,128)S(1)} %bitcast.313, f32[64,256]{1,0:T(8,128)S(1)} %copy-done.19), kind=kOutput, calls=%fused_computation.4 | convolution fusion | flops 100925440 | bytes 983040 | tf_op jit(solution)/shard_map/dot_general | solution.py:34
  (144 shorter events, 4.9 us)
Async XLA Ops:
  0.0 94.1 %copy-start = (f32[256,256]{1,0:T(8,128)S(1)}, f32[256,256]{1,0:T(8,128)}, u32[]{:S(2)}) copy-start(f32[256,256]{1,0:T(8,128)} %param.19) | copy-start | bytes 786436
  0.8 27.3 %collective-permute-start = (bf16[8,1,8,256]{3,2,1,0:T(8,128)(2,1)S(1)}, bf16[8,1,8,256]{3,2,1,0:T(8,128)(2,1)S(1)}, u32[]{:S(2)}, u32[]{:S(2)}) collective-permute-start(bf16[8,1,8,256]{3,2,1,0:T(8,128)(2,1)S(1)} %get-tuple-element.16), channel_id=1, source_target_pairs={{0,4},{4,8},{8,12},{12,16},{16,20},{20,24},{24,28},{1,5},{5,9},{9,... | collective-permute-start | bytes 98312 | tf_op jit(solution)/shard_map/ppermute | solution.py:20
  3.2 25.0 %collective-permute-start.1 = (bf16[8,1,8,256]{3,2,1,0:T(8,128)(2,1)S(1)}, bf16[8,1,8,256]{3,2,1,0:T(8,128)(2,1)S(1)}, u32[]{:S(2)}, u32[]{:S(2)}) collective-permute-start(bf16[8,1,8,256]{3,2,1,0:T(8,128)(2,1)S(1)} %get-tuple-element.15), channel_id=1, source_target_pairs={{4,0},{8,4},{12,8},{16,12},{20,16},{24,20},{28,24},{5,1},{9,5},{13... | collective-permute-start | bytes 98312 | tf_op jit(solution)/shard_map/ppermute | solution.py:22
  11.8 8.3 %copy-start.36 = (f32[2,8,8]{2,1,0:T(8,128)S(1)}, f32[2,8,8]{2,1,0:T(8,128)}, u32[]{:S(2)}) copy-start(f32[2,8,8]{2,1,0:T(8,128)} %param.17) | copy-start | bytes 1540
  11.8 8.9 %copy-start.44 = (s32[4,8,8]{2,1,0:T(8,128)S(1)}, s32[4,8,8]{2,1,0:T(8,128)}, u32[]{:S(2)}) copy-start(s32[4,8,8]{2,1,0:T(8,128)} %param.18) | copy-start | bytes 3076
  22.5 3.4 %copy-start.3 = (bf16[8,8,8,256]{3,2,1,0:T(8,128)(2,1)S(1)}, bf16[8,8,8,256]{3,2,1,0:T(8,128)(2,1)}, u32[]{:S(2)}) copy-start(bf16[8,8,8,256]{3,2,1,0:T(8,128)(2,1)} %param.16) | copy-start | bytes 786436
  28.3 11.5 %collective-permute-start.2 = (bf16[8,10,1,256]{3,2,1,0:T(2,128)(2,1)S(1)}, bf16[8,10,1,256]{3,2,1,0:T(2,128)(2,1)S(1)}, u32[]{:S(2)}, u32[]{:S(2)}) collective-permute-start(bf16[8,10,1,256]{3,2,1,0:T(2,128)(2,1)S(1)} %get-tuple-element.11), channel_id=1, source_target_pairs={{0,1},{1,2},{2,3},{4,5},{5,6},{6,7},{8,9},{9,10},{10,11},{12,13},{... | collective-permute-start | bytes 122888 | tf_op jit(solution)/shard_map/ppermute | solution.py:20
  32.5 7.3 %collective-permute-start.3 = (bf16[8,10,1,256]{3,2,1,0:T(2,128)(2,1)S(1)}, bf16[8,10,1,256]{3,2,1,0:T(2,128)(2,1)S(1)}, u32[]{:S(2)}, u32[]{:S(2)}) collective-permute-start(bf16[8,10,1,256]{3,2,1,0:T(2,128)(2,1)S(1)} %get-tuple-element.12), channel_id=1, source_target_pairs={{1,0},{2,1},{3,2},{5,4},{6,5},{7,6},{9,8},{10,9},{11,10},{13,12},{... | collective-permute-start | bytes 122888 | tf_op jit(solution)/shard_map/ppermute | solution.py:22
  46.2 2.9 %copy-start.1 = (f32[8,8,8,16,1]{4,3,2,1,0:T(8,128)S(1)}, f32[8,8,8,16,1]{4,3,2,1,0:T(8,128)}, u32[]{:S(2)}) copy-start(f32[8,8,8,16,1]{4,3,2,1,0:T(8,128)} %get-tuple-element.8) | copy-start | bytes 98308
  51.8 4.9 %copy-start.2 = (bf16[8,8,8,16,1]{4,3,0,2,1:T(8,128)(2,1)S(1)}, bf16[8,8,8,16,1]{4,3,0,2,1:T(8,128)(2,1)}, u32[]{:S(2)}) copy-start(bf16[8,8,8,16,1]{4,3,0,2,1:T(8,128)(2,1)} %slice.336) | copy-start | bytes 49156
  56.7 3.6 %copy-start.7 = (f32[8,8,8,16,1]{3,2,1,0,4:T(8,128)S(1)}, f32[8,8,8,16,1]{3,2,1,0,4:T(8,128)}, u32[]{:S(2)}) copy-start(f32[8,8,8,16,1]{3,2,1,0,4:T(8,128)} %copy.115) | copy-start | bytes 98308
  56.7 3.7 %copy-start.8 = (f32[8,8,8,1,16]{4,3,2,1,0:T(1,128)S(1)}, f32[8,8,8,1,16]{4,3,2,1,0:T(1,128)}, u32[]{:S(2)}) copy-start(f32[8,8,8,1,16]{4,3,2,1,0:T(1,128)} %get-tuple-element.5) | copy-start | bytes 98308
  56.7 5.1 %copy-start.4 = (bf16[8,8,8,256]{3,2,1,0:T(8,128)(2,1)S(1)}, bf16[8,8,8,256]{3,2,1,0:T(8,128)(2,1)}, u32[]{:S(2)}) copy-start(bf16[8,8,8,256]{3,2,1,0:T(8,128)(2,1)} %param.16) | copy-start | bytes 786436
  60.2 1.6 %copy-start.9 = (f32[8,8,8,512]{3,2,1,0:T(8,128)S(1)}, f32[8,8,8,512]{3,2,1,0:T(8,128)}, u32[]{:S(2)}) copy-start(f32[8,8,8,512]{3,2,1,0:T(8,128)} %convolution_bitcast_fusion) | copy-start | bytes 3145732
  60.2 1.6 %copy-start.38 = (pred[16,256]{1,0:T(8,128)(4,1)S(1)}, pred[16,256]{1,0:T(8,128)(4,1)}, u32[]{:S(2)}) copy-start(pred[16,256]{1,0:T(8,128)(4,1)} %get-tuple-element.59) | copy-start | bytes 12292
  60.2 1.6 %copy-start.39 = (pred[16,256]{1,0:T(8,128)(4,1)S(1)}, pred[16,256]{1,0:T(8,128)(4,1)}, u32[]{:S(2)}) copy-start(pred[16,256]{1,0:T(8,128)(4,1)} %get-tuple-element.60) | copy-start | bytes 12292
  60.2 1.6 %copy-start.40 = (pred[16,256]{1,0:T(8,128)(4,1)S(1)}, pred[16,256]{1,0:T(8,128)(4,1)}, u32[]{:S(2)}) copy-start(pred[16,256]{1,0:T(8,128)(4,1)} %get-tuple-element.61) | copy-start | bytes 12292
  60.2 1.6 %copy-start.41 = (pred[16,256]{1,0:T(8,128)(4,1)S(1)}, pred[16,256]{1,0:T(8,128)(4,1)}, u32[]{:S(2)}) copy-start(pred[16,256]{1,0:T(8,128)(4,1)} %get-tuple-element.62) | copy-start | bytes 12292
  60.2 1.6 %copy-start.42 = (f32[8,8]{1,0:T(8,128)S(1)}, f32[8,8]{1,0:T(8,128)}, u32[]{:S(2)}) copy-start(f32[8,8]{1,0:T(8,128)} %get-tuple-element.57) | copy-start | bytes 772
  60.2 1.6 %copy-start.43 = (f32[8,8]{1,0:T(8,128)S(1)}, f32[8,8]{1,0:T(8,128)}, u32[]{:S(2)}) copy-start(f32[8,8]{1,0:T(8,128)} %get-tuple-element.58) | copy-start | bytes 772
  60.4 2.1 %copy-start.22 = (f32[256,64]{0,1:T(8,128)S(1)}, f32[256,64]{0,1:T(8,128)}, u32[]{:S(2)}) copy-start(f32[256,64]{0,1:T(8,128)} %param.20) | copy-start | bytes 196612
  61.8 1.3 %copy-start.37 = (f32[128,64]{0,1:T(8,128)S(1)}, f32[128,64]{0,1:T(8,128)}, u32[]{:S(2)}) copy-start(f32[128,64]{0,1:T(8,128)} %param.22) | copy-start | bytes 98308
  61.9 1.7 %copy-start.21 = (f32[128,128]{1,0:T(8,128)S(1)}, f32[128,128]{1,0:T(8,128)}, u32[]{:S(2)}) copy-start(f32[128,128]{1,0:T(8,128)} %param.23) | copy-start | bytes 196612
  63.4 36.4 %copy-start.5 = (f32[9,256,256]{2,1,0:T(8,128)S(1)}, f32[9,256,256]{2,1,0:T(8,128)}, u32[]{:S(2)}) copy-start(f32[9,256,256]{2,1,0:T(8,128)} %param.30) | copy-start | bytes 7077892
  65.6 0.6 copy-start.10
  67.3 0.6 copy-start.12
  67.3 1.7 %copy-start.14 = (f32[8,1,2,128]{3,0,2,1:T(8,128)}, f32[8,1,2,128]{3,0,2,1:T(8,128)S(1)}, u32[]{:S(2)}) copy-start(f32[8,1,2,128]{3,0,2,1:T(8,128)S(1)} %get-tuple-element.40) | copy-start | bytes 24580
  69.0 0.6 copy-start.23
  69.0 2.3 %copy-start.25 = (f32[8,1,1,128]{3,0,2,1:T(8,128)}, f32[8,1,1,128]{3,0,2,1:T(8,128)S(1)}, u32[]{:S(2)}) copy-start(f32[8,1,1,128]{3,0,2,1:T(8,128)S(1)} %get-tuple-element.56) | copy-start | bytes 12292
  71.3 3.4 %collective-permute-start.4 = (f32[8,128]{1,0:T(8,128)}, f32[8,128]{1,0:T(8,128)}, u32[]{:S(2)}, u32[]{:S(2)}) collective-permute-start(f32[8,128]{1,0:T(8,128)} %fusion.65), channel_id=1, source_target_pairs={{0,4},{4,0},{8,12},{12,8},{16,20},{20,16},{24,28},{28,24},{1,5},{5... | collective-permute-start | bytes 12296 | tf_op jit(solution)/shard_map/ppermute | solution.py:30
  75.3 0.6 copy-start.27
  75.3 2.3 %copy-start.29 = (f32[8,128]{1,0:T(8,128)}, f32[8,128]{1,0:T(8,128)S(1)}, u32[]{:S(2)}) copy-start(f32[8,128]{1,0:T(8,128)S(1)} %get-tuple-element.54) | copy-start | bytes 12292
  77.6 4.1 %collective-permute-start.5 = (f32[8,128]{1,0:T(8,128)}, f32[8,128]{1,0:T(8,128)}, u32[]{:S(2)}, u32[]{:S(2)}) collective-permute-start(f32[8,128]{1,0:T(8,128)} %fusion.63), channel_id=1, source_target_pairs={{0,8},{4,12},{8,0},{12,4},{16,24},{20,28},{24,16},{28,20},{1,9},{5... | collective-permute-start | bytes 12296 | tf_op jit(solution)/shard_map/ppermute | solution.py:30
  82.4 0.6 copy-start.31
  82.4 2.3 %copy-start.33 = (f32[8,128]{1,0:T(8,128)}, f32[8,128]{1,0:T(8,128)S(1)}, u32[]{:S(2)}) copy-start(f32[8,128]{1,0:T(8,128)S(1)} %get-tuple-element.52) | copy-start | bytes 12292
  84.7 4.5 %collective-permute-start.6 = (f32[8,128]{1,0:T(8,128)}, f32[8,128]{1,0:T(8,128)}, u32[]{:S(2)}, u32[]{:S(2)}) collective-permute-start(f32[8,128]{1,0:T(8,128)} %fusion.61), channel_id=1, source_target_pairs={{0,1},{1,0},{2,3},{3,2},{4,5},{5,4},{6,7},{7,6},{8,9},{9,8},{10,11... | collective-permute-start | bytes 12296 | tf_op jit(solution)/shard_map/ppermute | solution.py:30
  87.4 15.1 %copy-start.20 = (f32[128,128]{1,0:T(8,128)S(1)}, f32[128,128]{1,0:T(8,128)}, u32[]{:S(2)}) copy-start(f32[128,128]{1,0:T(8,128)} %param.31) | copy-start | bytes 196612
  87.4 15.3 %copy-start.6 = (f32[9,128,256]{2,1,0:T(8,128)S(1)}, f32[9,128,256]{2,1,0:T(8,128)}, u32[]{:S(2)}) copy-start(f32[9,128,256]{2,1,0:T(8,128)} %param.27) | copy-start | bytes 3538948
  87.4 16.7 %copy-start.32 = (f32[8,128]{1,0:T(8,128)S(1)}, f32[8,128]{1,0:T(8,128)}, u32[]{:S(2)}) copy-start(f32[8,128]{1,0:T(8,128)} %copy-done.31) | copy-start | bytes 12292
  87.4 16.7 %copy-start.34 = (f32[8,128]{1,0:T(8,128)S(1)}, f32[8,128]{1,0:T(8,128)}, u32[]{:S(2)}) copy-start(f32[8,128]{1,0:T(8,128)} %copy-done.33) | copy-start | bytes 12292
  87.4 17.1 %copy-start.28 = (f32[8,128]{1,0:T(8,128)S(1)}, f32[8,128]{1,0:T(8,128)}, u32[]{:S(2)}) copy-start(f32[8,128]{1,0:T(8,128)} %copy-done.27) | copy-start | bytes 12292
  87.4 17.1 %copy-start.30 = (f32[8,128]{1,0:T(8,128)S(1)}, f32[8,128]{1,0:T(8,128)}, u32[]{:S(2)}) copy-start(f32[8,128]{1,0:T(8,128)} %copy-done.29) | copy-start | bytes 12292
  91.0 13.9 %copy-start.24 = (f32[8,1,1,128]{3,0,2,1:T(8,128)S(1)}, f32[8,1,1,128]{3,0,2,1:T(8,128)}, u32[]{:S(2)}) copy-start(f32[8,1,1,128]{3,0,2,1:T(8,128)} %copy-done.23) | copy-start | bytes 12292
  91.0 13.9 %copy-start.26 = (f32[8,1,1,128]{3,0,2,1:T(8,128)S(1)}, f32[8,1,1,128]{3,0,2,1:T(8,128)}, u32[]{:S(2)}) copy-start(f32[8,1,1,128]{3,0,2,1:T(8,128)} %copy-done.25) | copy-start | bytes 12292
  91.0 4.7 %collective-permute-start.7 = (f32[8,128]{1,0:T(8,128)S(1)}, f32[8,128]{1,0:T(8,128)S(1)}, u32[]{:S(2)}, u32[]{:S(2)}) collective-permute-start(f32[8,128]{1,0:T(8,128)S(1)} %fusion.59), channel_id=1, source_target_pairs={{0,16},{4,20},{8,24},{12,28},{16,0},{20,4},{24,8},{28,12},{1,17},{... | collective-permute-start | bytes 12296 | tf_op jit(solution)/shard_map/ppermute | solution.py:30
  94.7 10.6 %copy-start.13 = (f32[8,1,2,128]{3,0,2,1:T(8,128)S(1)}, f32[8,1,2,128]{3,0,2,1:T(8,128)}, u32[]{:S(2)}) copy-start(f32[8,1,2,128]{3,0,2,1:T(8,128)} %copy-done.12) | copy-start | bytes 24580
  94.7 10.6 %copy-start.15 = (f32[8,1,2,128]{3,0,2,1:T(8,128)S(1)}, f32[8,1,2,128]{3,0,2,1:T(8,128)}, u32[]{:S(2)}) copy-start(f32[8,1,2,128]{3,0,2,1:T(8,128)} %copy-done.14) | copy-start | bytes 24580
  94.7 11.0 %copy-start.11 = (f32[8,2,2,128]{3,0,2,1:T(8,128)S(1)}, f32[8,2,2,128]{3,0,2,1:T(8,128)}, u32[]{:S(2)}) copy-start(f32[8,2,2,128]{3,0,2,1:T(8,128)} %copy-done.10) | copy-start | bytes 49156
  96.8 4.6 %collective-permute-start.8 = (f32[8,128]{1,0:T(8,128)S(1)}, f32[8,128]{1,0:T(8,128)S(1)}, u32[]{:S(2)}, u32[]{:S(2)}) collective-permute-start(f32[8,128]{1,0:T(8,128)S(1)} %fusion.57), channel_id=1, source_target_pairs={{0,2},{1,3},{2,0},{3,1},{4,6},{5,7},{6,4},{7,5},{8,10},{9,11},{10,... | collective-permute-start | bytes 12296 | tf_op jit(solution)/shard_map/ppermute | solution.py:30
  103.0 3.3 %copy-start.16 = (f32[128,128]{1,0:T(8,128)S(1)}, f32[128,128]{1,0:T(8,128)}, u32[]{:S(2)}) copy-start(f32[128,128]{1,0:T(8,128)} %param.26) | copy-start | bytes 196612
  103.2 3.3 %copy-start.17 = (f32[128,128]{1,0:T(8,128)S(1)}, f32[128,128]{1,0:T(8,128)}, u32[]{:S(2)}) copy-start(f32[128,128]{1,0:T(8,128)} %param.29) | copy-start | bytes 196612
  104.3 2.7 %copy-start.35 = (f32[64,128]{1,0:T(8,128)S(1)}, f32[64,128]{1,0:T(8,128)}, u32[]{:S(2)}) copy-start(f32[64,128]{1,0:T(8,128)} %param.25) | copy-start | bytes 98308
  104.5 2.7 %copy-start.18 = (f32[128,128]{1,0:T(8,128)S(1)}, f32[128,128]{1,0:T(8,128)}, u32[]{:S(2)}) copy-start(f32[128,128]{1,0:T(8,128)} %param.28) | copy-start | bytes 196612
  106.3 1.4 %copy-start.19 = (f32[64,256]{1,0:T(8,128)S(1)}, f32[64,256]{1,0:T(8,128)}, u32[]{:S(2)}) copy-start(f32[64,256]{1,0:T(8,128)} %param.21) | copy-start | bytes 196612
where the time goes:
time: 110 us; the launch traced here: 109 us
  local copies, waits for them, and re-layouts  47.2 us (43%)
  starting transfers between devices  22.4 us (20%)
  matrix products  22.2 us (20%)
  other arithmetic  9.76 us (9%)
  waiting for transfers between devices  6.47 us (6%)
    dot_general x39, matrix products, product(): jnp.dot(left, right, precision=highest, preferred_element_type=jnp.float32)  22.2 us
    ppermute x5, starting transfers between devices, from_partner(): lax.ppermute(array, axis, [(i, i ^ 1 << stride) for i in range(lax.axis_s...  13.2 us
    unnamed x96, local copies, waits for them, and re-layouts  12.9 us
    slice x1, local copies, waits for them, and re-layouts, edge_values(): node_grid[..., :, 0]  8.21 us
    ppermute x2, starting transfers between devices, padded_2(): lax.ppermute(tail, axis, [(i, (i + 1) % count) for i in range(ends)])  6.61 us
    ppermute x5, waiting for transfers between devices, from_partner(): lax.ppermute(array, axis, [(i, i ^ 1 << stride) for i in range(lax.axis_s...  6.46 us
    sub x1, local copies, waits for them, and re-layouts, forcing_term(): neighbours[side_index] - own_edges[side_index]  4.86 us
    reshape x1, local copies, waits for them, and re-layouts, edge_values(): tracer_field.reshape(tracer_field.shape[:-1] + (node_count, node_count))  3.68 us
  transfers between devices with their start and end apart: 9, of which 5 were waited for; matrix products, arithmetic and copies ran while one was open for 29% of the time, Pallas kernels for 0%

commit v1 on v0

v1 whole, which is shorter than its diff:
```python
import functools

import jax
import jax.numpy as jnp
import numpy as np
from jax import lax
from jax.experimental import pallas as pl
from jax.experimental.pallas import tpu as pltpu
from jax.sharding import PartitionSpec as P

NODE = 16
SQUARE = NODE * NODE
F32 = jnp.float32
BF16 = jnp.bfloat16
MESH = pl.DeviceIdType.MESH


def local_plan(leaf_side):
    merge_plan = []
    block_span = leaf_side
    while block_span > 1:
        merge_plan = merge_plan + [1, 2]
        block_span = block_span // 2
    return merge_plan


def cross_plan(count_first, count_second):
    merge_plan = []
    bits = {"gx": 0, "gy": 0}
    while count_first * count_second > 1:
        if count_first >= count_second:
            axis, count_first = "gx", count_first // 2
        else:
            axis, count_second = "gy", count_second // 2
        merge_plan.append((axis, bits[axis]))
        bits[axis] += 1
    return merge_plan


def staged(plan):
    stages, start, size = [], 0, 2
    while start < len(plan):
        stages.append(plan[start : start + size])
        start, size = start + size, 3
    return stages


def point_tables():
    index = np.arange(NODE)
    points = -np.cos(np.pi * index / (NODE - 1))
    weights = np.where(index % 2 == 0, 1.0, -1.0)
    weights[[0, NODE - 1]] *= 2.0
    eye = np.eye(NODE)
    matrix = weights[:, None] / weights[None, :] / (points[:, None] - points[None, :] + eye)
    matrix = matrix * (1.0 - eye)
    matrix = matrix - np.diag(matrix.sum(axis=1))
    both = np.concatenate([np.kron(matrix, eye).T, np.kron(eye, matrix).T], axis=1)
    both = both.astype(np.float32)
    high = both.astype(jnp.bfloat16)
    low = (both - high.astype(np.float32)).astype(jnp.bfloat16)
    facing = np.zeros((SQUARE, 2 * SQUARE), np.float32)
    last = NODE - 1
    for k in range(NODE):
        facing[last * NODE + k, k] = 1.0
        facing[k, last * NODE + k] = 1.0
        facing[k * NODE + last, SQUARE + k * NODE] = 1.0
        facing[k * NODE, SQUARE + k * NODE + last] = 1.0
    return np.concatenate([high, low, facing.astype(jnp.bfloat16)], axis=1)


def split(x):
    high = x.astype(BF16)
    return high, (x - high.astype(F32)).astype(BF16)


def dot(left, right):
    return jnp.dot(left, right, preferred_element_type=F32)


def product(x, weight):
    high, low = weight
    rows = x.shape[0]
    if rows >= 64:
        x_high, x_low = split(x)
        return dot(x_high, high) + dot(x_low, high) + dot(x_high, low)
    rest = x - x.astype(BF16).astype(F32)
    both = jnp.concatenate([x, rest], axis=0).astype(BF16)
    out = dot(both, high) + dot(both, low)
    return out[:rows] + out[rows:]


def lanes(shape):
    return lax.broadcasted_iota(jnp.int32, shape, len(shape) - 1)


def left_half(shape):
    return lanes(shape) < shape[-1] // 2


def kernel(stages, leaf_side, tracer_count, *refs):
    names = ["u", "velocity", "inflow", "tables", "leaf_solve", "leaf_skeleton", "leaf_lift"]
    names += [a + "_" + b for a in ("merge", "parent", "sibling") for b in ("first", "second", "rest")]
    names += ["root_map"]
    hbm = dict(zip(names, refs[: len(names)]))
    out_ref = refs[len(names)]
    rest = refs[len(names) + 1 :]
    v = dict(zip(names, rest[: len(names)]))
    (
        load_sem, force, near, w_second, level_one, down_one, solved, t0_ref, t1_ref,
        up_high, up_low, par_high, par_low,
        send_x, send_y, halo_x, halo_y, halo_send, halo_recv,
    ) = rest[len(names) : len(names) + 19]
    stage_refs = rest[len(names) + 19 :]
    T, L = tracer_count, leaf_side
    leaves = L * L
    rows = T * leaves

    loads = {}
    for k, name in enumerate(names):
        loads[name] = pltpu.make_async_copy(hbm[name], v[name], load_sem.at[k])
    order = ["u", "tables", "velocity", "inflow", "leaf_skeleton"]
    order += ["merge_first", "merge_second", "merge_rest", "leaf_solve"]
    order += ["sibling_first", "sibling_second", "sibling_rest", "parent_rest", "root_map"]
    order += ["parent_second", "parent_first", "leaf_lift"]
    for name in order:
        loads[name].start()

    place = {"gx": lax.axis_index("gx"), "gy": lax.axis_index("gy")}
    count = {"gx": lax.axis_size("gx"), "gy": lax.axis_size("gy")}
    bit_of = lambda axis, bit: lax.rem(place[axis] // (1 << bit), 2)

    def partner(stage, mask):
        target = dict(place)
        for k, (axis, bit) in enumerate(stage):
            if mask >> (len(stage) - 1 - k) & 1:
                target[axis] = target[axis] + (1 - 2 * bit_of(axis, bit)) * (1 << bit)
        return (target["gx"], target["gy"])

    barrier = pltpu.get_barrier_semaphore()
    expected = jnp.int32(0)
    for stage in stages:
        for mask in range(1, 1 << len(stage)):
            pl.semaphore_signal(barrier, inc=1, device_id=partner(stage, mask), device_id_type=MESH)
            expected = expected + 1
    has, beside = {}, {}
    for axis in ("gx", "gy"):
        for way in (-1, 1):
            spot = dict(place)
            spot[axis] = spot[axis] + way
            beside[axis, way] = (spot["gx"], spot["gy"])
            has[axis, way] = place[axis] > 0 if way < 0 else place[axis] < count[axis] - 1

            @pl.when(has[axis, way])
            def _(axis=axis, way=way):
                pl.semaphore_signal(barrier, inc=1, device_id=beside[axis, way], device_id_type=MESH)

            expected = expected + jnp.where(has[axis, way], 1, 0)

    loads["u"].wait()
    loads["tables"].wait()
    u = v["u"][...].astype(F32).reshape(rows, SQUARE)
    ub = u.astype(BF16)
    facing = dot(ub, v["tables"][:, 4 * SQUARE :])
    for c in range(4):
        near[c * rows : (c + 1) * rows, :] = facing[:, c * 128 : (c + 1) * 128]
    for t in range(T):
        base = t * leaves
        send_x[1, t * L : (t + 1) * L, :] = facing[base + leaves - L : base + leaves, :128]
        send_x[0, t * L : (t + 1) * L, :] = facing[base : base + L, 128:256]
    for k in range(2):
        for c in range(2):
            line = pl.ds((2 + c) * rows + k * (L - 1), T * L, stride=L)
            send_y[k, c * T * L : (c + 1) * T * L, :] = near[line, :]
    pl.semaphore_wait(barrier, expected)

    def halo_copy(axis, way):
        k = 0 if way < 0 else 1
        source, target = (send_x, halo_x) if axis == "gx" else (send_y, halo_y)
        slot = k + (0 if axis == "gx" else 2)
        return pltpu.make_async_remote_copy(
            src_ref=source.at[k],
            dst_ref=target.at[k],
            send_sem=halo_send.at[slot],
            recv_sem=halo_recv.at[slot],
            device_id=beside[axis, way],
            device_id_type=MESH,
        )

    sides = [("gy", -1), ("gy", 1), ("gx", -1), ("gx", 1)]
    for axis, way in sides:

        @pl.when(has[axis, way])
        def _(axis=axis, way=way):
            halo_copy(axis, way).start()

    loads["velocity"].wait()
    loads["inflow"].wait()
    own = lax.broadcasted_iota(jnp.int32, (leaves, L), 0) % L == lanes((leaves, L))

    def column(grid):
        wide = jnp.concatenate(
            [jnp.broadcast_to(grid[i : i + 1, :], (L, L)) for i in range(L)], axis=0
        )
        return jnp.sum(jnp.where(own, wide, 0.0), axis=1, keepdims=True)

    speed = [v["velocity"][k] for k in range(2)]
    strength = [
        column(v["inflow"][s].astype(F32) * (NODE * jnp.abs(speed[s // 2]))) for s in range(4)
    ]
    half = (leaves, SQUARE // 2)
    full = (leaves, SQUARE)
    weight_0 = jnp.where(lanes(half) < NODE, strength[0], 0.0)
    weight_1 = jnp.where(lanes(half) >= SQUARE // 2 - NODE, strength[1], 0.0)
    weight_2 = jnp.where(lanes(full) % NODE == 0, strength[2], 0.0)
    weight_3 = jnp.where(lanes(full) % NODE == NODE - 1, strength[3], 0.0)
    for k, weight in enumerate((weight_2, weight_3)):
        for c in range(2):
            at = (2 * k + c) * leaves
            w_second[at : at + leaves, :] = weight[:, c * 128 : (c + 1) * 128]
    keep = 1.0 - (jnp.concatenate([weight_0, weight_1], axis=1) + weight_2 + weight_3)
    spot = lax.broadcasted_iota(jnp.int32, full, 0) % L
    inner_2 = jnp.where(spot == 0, 0.0, weight_2)
    inner_3 = jnp.where(spot == L - 1, 0.0, weight_3)
    speed_0, speed_1 = column(speed[0]), column(speed[1])
    grads = dot(ub, v["tables"][:, : 2 * SQUARE]) + dot(ub, v["tables"][:, 2 * SQUARE : 4 * SQUARE])
    empty = jnp.zeros((L, SQUARE // 2), F32)
    for t in range(T):
        low, top = t * leaves, (t + 1) * leaves
        own_u = u[low:top]
        own_first = facing[low:top, :SQUARE]
        own_second = facing[low:top, SQUARE:].reshape(L, L, SQUARE)
        from_0 = jnp.concatenate([empty, own_first[: leaves - L, : SQUARE // 2]], axis=0)
        from_1 = jnp.concatenate([own_first[L:, SQUARE // 2 :], empty], axis=0)
        from_2 = pltpu.roll(own_second, 1, 1).reshape(leaves, SQUARE)
        from_3 = pltpu.roll(own_second, L - 1, 1).reshape(leaves, SQUARE)
        first = jnp.concatenate([weight_0 * from_0, weight_1 * from_1], axis=1)
        total = (
            keep * own_u
            - speed_0 * grads[low:top, :SQUARE]
            - speed_1 * grads[low:top, SQUARE:]
            + first
            + inner_2 * from_2
            + inner_3 * from_3
        )
        for c in range(2):
            force[c * rows + low : c * rows + top, :] = total[:, c * 128 : (c + 1) * 128]

    for name in ("leaf_skeleton", "merge_first", "merge_second", "merge_rest"):
        loads[name].wait()
    depth = v["merge_rest"].shape[0]
    for k in range(depth):
        up_high[k], up_low[k] = split(v["merge_rest"][k])
    up = lambda k: (up_high[k], up_low[k])
    twice = lambda w, axis: jnp.concatenate([w, w], axis=axis)
    w_skeleton = split(twice(v["leaf_skeleton"][...], 1))
    w_first = split(twice(v["merge_first"][...], 1))
    w_merge_second = split(v["merge_second"][...])

    for axis, way in sides:

        @pl.when(has[axis, way])
        def _(axis=axis, way=way):
            k = 0 if way < 0 else 1
            halo_copy(axis, way).wait_send()
            halo_copy(axis, -way).wait_recv()
            arrived = (halo_x if axis == "gx" else halo_y)[1 - k]
            if axis == "gx":
                edge = 0 if way < 0 else leaves - L
                weight = weight_0[:L] if way < 0 else weight_1[leaves - L :]
                for t in range(T):
                    start = k * rows + t * leaves + edge
                    at = slice(start, start + L)
                    force[at, :] = force[at, :] + weight * arrived[t * L : (t + 1) * L]
            else:
                edge = 0 if way < 0 else L - 1
                for c in range(2):
                    weight = w_second[pl.ds((2 * k + c) * leaves + edge, L, stride=L), :]
                    weight = jnp.concatenate([weight] * T, axis=0)
                    at = pl.ds(c * rows + edge, T * L, stride=L)
                    line = arrived[c * T * L : (c + 1) * T * L]
                    force[at, :] = force[at, :] + weight * line

    forcing = jnp.concatenate([force[:rows, :], force[rows:, :]], axis=1)
    skeleton = product(forcing, w_skeleton).reshape(T, L // 2, 2, L, 128)
    pair = (T * leaves // 2, 128)
    cat_0 = jnp.where(
        left_half(pair), skeleton[:, :, 0].reshape(pair), skeleton[:, :, 1].reshape(pair)
    )
    level_one[...] = product(cat_0, w_first)
    boxes = [
        (a + 2 * c, b + 2 * d) for a in range(2) for b in range(2) for c in range(2) for d in range(2)
    ]
    stride = leaves // 2
    at_box = lambda i, j: pl.ds(i * L + j, T, stride=stride)
    is_left = left_half((T, 128))
    cat_1 = jnp.concatenate(
        [
            jnp.where(is_left, level_one[at_box(i, 2 * j), :], level_one[at_box(i, 2 * j + 1), :])
            for i, j in boxes
        ],
        axis=0,
    )
    current = product(cat_1, w_merge_second)

    def joined(x):
        middle = x.shape[0] // 2
        return jnp.concatenate([x[:middle], x[middle:]], axis=1)

    cats = []
    for k in range(4):
        cats.append(joined(current))
        current = product(cats[-1], up(k))

    level = 4
    path = []
    for number, stage in enumerate(stages):
        pool, stage_send, stage_recv = stage_refs[3 * number : 3 * number + 3]
        slots = 1 << len(stage)
        own_slot = jnp.int32(0)
        for axis, bit in stage:
            own_slot = own_slot * 2 + bit_of(axis, bit)
        pool[own_slot] = current
        copies = [
            pltpu.make_async_remote_copy(
                src_ref=pool.at[own_slot],
                dst_ref=pool.at[own_slot],
                send_sem=stage_send.at[mask],
                recv_sem=stage_recv.at[mask],
                device_id=partner(stage, mask),
                device_id_type=MESH,
            )
            for mask in range(1, slots)
        ]
        for copy in reversed(copies):
            copy.start()
        if number == 0:
            for name in ("leaf_solve", "sibling_first", "sibling_second", "sibling_rest"):
                loads[name].wait()
            local_terms = [product(cats[k], split(v["sibling_rest"][k])) for k in range(4)]
            t1_ref[...] = product(cat_1, split(v["sibling_second"][...]))
            t0_ref[...] = product(cat_0, split(v["sibling_first"][...]))
        if number == len(stages) - 1:
            solved[...] = product(forcing, split(v["leaf_solve"][...]))
            for name in ("parent_rest", "root_map", "parent_second", "parent_first", "leaf_lift"):
                loads[name].wait()
            for k in range(depth):
                par_high[k], par_low[k] = split(v["parent_rest"][k])
            w_root = split(v["root_map"][...])
            w_parent_second = split(v["parent_second"][...])
            w_parent_first = split(twice(v["parent_first"][...], 0))
            w_lift = split(twice(v["leaf_lift"][...], 0))
        for copy in copies:
            copy.wait()
        current = pool[...].reshape(slots * T, 128)
        for k, (axis, bit) in enumerate(stage):
            cat = joined(current)
            mine = cat
            for later_axis, later_bit in stage[k + 1 :]:
                middle = mine.shape[0] // 2
                mine = jnp.where(bit_of(later_axis, later_bit) == 1, mine[middle:], mine[:middle])
            path.append((level, bit_of(axis, bit), product(mine, split(v["sibling_rest"][level]))))
            current = product(cat, up(level))
            level += 1

    down = lambda k: (par_high[k], par_low[k])
    boundary = product(current, w_root)
    for level, bit, term in reversed(path):
        both = product(boundary, down(level)) + term
        boundary = jnp.where(bit == 1, both[:, 128:], both[:, :128])
    for k in reversed(range(4)):
        both = product(boundary, down(k)) + local_terms[k]
        boundary = jnp.concatenate([both[:, :128], both[:, 128:]], axis=0)
    both = product(boundary, w_parent_second) + t1_ref[...]
    for k, (i, j) in enumerate(boxes):
        one = both[k * T : (k + 1) * T]
        down_one[at_box(i, 2 * j), :] = jnp.where(is_left, one, 0.0)
        down_one[at_box(i, 2 * j + 1), :] = jnp.where(is_left, 0.0, one)
    both = product(down_one[...], w_parent_first) + t0_ref[...]
    split_left = left_half(pair)
    shape = (T, L // 2, 1, L, 128)
    leaf_boundary = jnp.concatenate(
        [
            jnp.where(split_left, both, 0.0).reshape(shape),
            jnp.where(split_left, 0.0, both).reshape(shape),
        ],
        axis=2,
    ).reshape(rows, 128)
    updated = solved[...] + product(leaf_boundary, w_lift)
    out_ref[...] = updated.reshape(out_ref.shape).astype(out_ref.dtype)


def local(tables, count_first, count_second, tracers, *operands):
    T, L = tracers.shape[0], tracers.shape[1]
    assert L == 8 and local_plan(L) == [1, 2] * 3
    stages = staged(cross_plan(count_first, count_second))
    rows = T * L * L
    args = (tracers, operands[0], operands[1], tables) + operands[2:]
    depth = operands[7].shape[0]
    vmem, dma = pltpu.VMEM, pltpu.SemaphoreType.DMA
    scratch = [vmem(a.shape, a.dtype) for a in args]
    scratch += [
        dma((len(args),)),
        vmem((2 * rows, 128), F32),
        vmem((4 * rows, 128), F32),
        vmem((4 * L * L, 128), F32),
        vmem((rows // 2, 128), F32),
        vmem((rows // 2, 128), F32),
        vmem((rows, SQUARE), F32),
        vmem((rows // 2, 128), F32),
        vmem((rows // 4, 128), F32),
        vmem((depth, 256, 128), BF16),
        vmem((depth, 256, 128), BF16),
        vmem((depth, 128, 256), BF16),
        vmem((depth, 128, 256), BF16),
        vmem((2, T * L, 128), F32),
        vmem((2, 2 * T * L, 128), F32),
        vmem((2, T * L, 128), F32),
        vmem((2, 2 * T * L, 128), F32),
        dma((4,)),
        dma((4,)),
    ]
    for stage in stages:
        slots = 1 << len(stage)
        scratch += [vmem((slots, T, 128), F32), dma((slots,)), dma((slots,))]
    return pl.pallas_call(
        functools.partial(kernel, stages, L, T),
        out_shape=jax.ShapeDtypeStruct(tracers.shape, tracers.dtype),
        in_specs=[pl.BlockSpec(memory_space=pl.ANY)] * len(args),
        out_specs=pl.BlockSpec(memory_space=pltpu.VMEM),
        scratch_shapes=scratch,
        compiler_params=pltpu.CompilerParams(
            collective_id=0, has_side_effects=True, vmem_limit_bytes=60 * 1024 * 1024
        ),
    )(*args)


def solution(mesh):
    tables = point_tables()
    split_both = P(None, "gx", "gy")
    in_specs = (P(None, "gx", "gy", None), split_both, split_both) + (P(),) * 13

    def body(*args):
        return local(
            jnp.asarray(tables), mesh.shape["gx"], mesh.shape["gy"], *args
        )

    return jax.shard_map(
        body,
        mesh=mesh,
        in_specs=in_specs,
        out_specs=P(None, "gx", "gy", None),
        check_vma=False,
    )
```

time: 110 us -> 27.6 us (0.25)
  local copies, waits for them, and re-layouts: 47.2 us -> 4.74 us
  Pallas kernels: 0 us -> 22.6 us
  starting transfers between devices: 22.4 us -> 0 us
  matrix products: 22.2 us -> 0 us
  other arithmetic: 9.76 us -> 0 us
  waiting for transfers between devices: 6.47 us -> 0 us
    pallas_call x0 -> x1, Pallas kernels: none -> 22.6 us  [local(): pl.pallas_call(functools.partial(kernel, stages, L, T), out_shape=jax.Sha...]
    ppermute x9 -> x0, starting transfers between devices: 22.4 us -> none  [the longest x5 13.2 us: from_partner(): lax.ppermute(array, axis, [(i, i ^ 1 << stride) for i in range(lax.axis_s...]
    dot_general x39 -> x0, matrix products: 22.2 us -> none  [product(): jnp.dot(left, right, precision=highest, preferred_element_type=jnp.float32)]
    slice x8 -> x0, local copies, waits for them, and re-layouts: 16.8 us -> none  [the longest x1 8.21 us: edge_values(): node_grid[..., :, 0]]
    unnamed x96 -> x3, local copies, waits for them, and re-layouts: 12.9 us -> 4.74 us
    reshape x2 -> x0, local copies, waits for them, and re-layouts: 7.26 us -> none  [the longest x1 3.68 us: edge_values(): tracer_field.reshape(tracer_field.shape[:-1] + (node_count, node_count))]
    ppermute x9 -> x0, waiting for transfers between devices: 6.47 us -> none  [the longest x5 6.46 us: from_partner(): lax.ppermute(array, axis, [(i, i ^ 1 << stride) for i in range(lax.axis_s...]
    sub x1 -> x0, local copies, waits for them, and re-layouts: 4.86 us -> none  [forcing_term(): neighbours[side_index] - own_edges[side_index]]
  transfers between devices with their start and end apart: 9 -> 0, of which waited for: 5 -> 0; matrix products, arithmetic and copies ran while one was open for 29% -> 0% of each run, Pallas kernels for 0% -> 0%
where the time goes in v1:
time: 27.6 us; the launch traced here: 27.3 us
  Pallas kernels  22.6 us (82%)
  local copies, waits for them, and re-layouts  4.74 us (17%)
    pallas_call x1, Pallas kernels, local(): pl.pallas_call(functools.partial(kernel, stages, L, T), out_shape=jax.Sha...  22.6 us
    unnamed x3, local copies, waits for them, and re-layouts  4.74 us

profile of v1, /device:TPU:0, one launch (start us, length us, event | category | flops | bytes accessed | tf_op | source)
XLA Modules:
  0.0 27.3 jit_solution(15876476427796824547)
XLA Ops:
  0.0 1.5 %copy.19.refs_7_ = f32[128,64]{1,0:T(8,128)} copy(f32[128,64]{0,1:T(8,128)} %param.23) | data formatting | bytes 65536 | tf_op args[6]
  1.5 1.6 %copy.18.refs_5_ = f32[256,64]{1,0:T(8,128)} copy(f32[256,64]{0,1:T(8,128)} %param.21) | data formatting | bytes 131072 | tf_op args[4]
  3.1 22.6 %shard_map.163 = bf16[8,8,8,256]{3,2,1,0:T(8,128)(2,1)} custom-call(bf16[8,8,8,256]{3,2,1,0:T(8,128)(2,1)} %refs_0_.1, f32[2,8,8]{2,1,0:T(8,128)} %refs_1_.1, s32[4,8,8]{2,1,0:T(8,128)} %refs_2_.1, bf16[256,1536]{1,0:T(8,128)(2,1)} %constant.2.clone.refs_3_, f32[256,256]{1,0:T(8,128)} %refs_4_.1, f32[256,64]{1,0:T(8,128)} %copy.18.refs_5_, ...), custom_call_target="tpu_custom_call" | custom-call | tf_op jit(solution)/shard_map/pallas_call | solution.py:425
  25.7 1.7 %copy.21 = bf16[8,8,8,256]{3,2,1,0:T(8,128)(2,1)} copy(bf16[8,8,8,256]{3,2,1,0:T(8,128)(2,1)} %shard_map.163) | data formatting | bytes 524288

commit v2 on v1

--- a/solution.py
+++ b/solution.py
@@ -12,6 +12,7 @@
 SQUARE = NODE * NODE
 F32 = jnp.float32
 BF16 = jnp.bfloat16
+VMEM_LIMIT = 60 * 1024 * 1024
 MESH = pl.DeviceIdType.MESH
 
 
@@ -77,7 +78,11 @@
     return jnp.dot(left, right, preferred_element_type=F32)
 
 
-def product(x, weight):
+def dot_across(left, right):
+    return lax.dot_general(left, right, (((1,), (1,)), ((), ())), preferred_element_type=F32)
+
+
+def product(x, weight, dot=dot):
     high, low = weight
     rows = x.shape[0]
     if rows >= 64:
@@ -252,8 +257,8 @@
         up_high[k], up_low[k] = split(v["merge_rest"][k])
     up = lambda k: (up_high[k], up_low[k])
     twice = lambda w, axis: jnp.concatenate([w, w], axis=axis)
-    w_skeleton = split(twice(v["leaf_skeleton"][...], 1))
-    w_first = split(twice(v["merge_first"][...], 1))
+    w_skeleton = split(twice(v["leaf_skeleton"][...], 0))
+    w_first = split(twice(v["merge_first"][...], 0))
     w_merge_second = split(v["merge_second"][...])
 
     for axis, way in sides:
@@ -281,12 +286,12 @@
                     force[at, :] = force[at, :] + weight * line
 
     forcing = jnp.concatenate([force[:rows, :], force[rows:, :]], axis=1)
-    skeleton = product(forcing, w_skeleton).reshape(T, L // 2, 2, L, 128)
+    skeleton = product(forcing, w_skeleton, dot_across).reshape(T, L // 2, 2, L, 128)
     pair = (T * leaves // 2, 128)
     cat_0 = jnp.where(
         left_half(pair), skeleton[:, :, 0].reshape(pair), skeleton[:, :, 1].reshape(pair)
     )
-    level_one[...] = product(cat_0, w_first)
+    level_one[...] = product(cat_0, w_first, dot_across)
     boxes = [
         (a + 2 * c, b + 2 * d) for a in range(2) for b in range(2) for c in range(2) for d in range(2)
     ]
@@ -394,7 +399,8 @@
     assert L == 8 and local_plan(L) == [1, 2] * 3
     stages = staged(cross_plan(count_first, count_second))
     rows = T * L * L
-    args = (tracers, operands[0], operands[1], tables) + operands[2:]
+    args = [tracers, operands[0], operands[1], tables] + list(operands[2:])
+    args[5], args[7] = args[5].T, args[7].T
     depth = operands[7].shape[0]
     vmem, dma = pltpu.VMEM, pltpu.SemaphoreType.DMA
     scratch = [vmem(a.shape, a.dtype) for a in args]
@@ -429,7 +435,7 @@
         out_specs=pl.BlockSpec(memory_space=pltpu.VMEM),
         scratch_shapes=scratch,
         compiler_params=pltpu.CompilerParams(
-            collective_id=0, has_side_effects=True, vmem_limit_bytes=60 * 1024 * 1024
+            collective_id=0, has_side_effects=True, vmem_limit_bytes=VMEM_LIMIT
         ),
     )(*args)
 

time: 27.6 us -> 24.4 us (0.88)
  local copies, waits for them, and re-layouts: 4.74 us -> 1.67 us
    unnamed x3 -> x1, local copies, waits for them, and re-layouts: 4.74 us -> 1.67 us
where the time goes in v2:
time: 24.4 us; the launch traced here: 24.3 us
  Pallas kernels  22.6 us (93%)
  local copies, waits for them, and re-layouts  1.67 us (7%)
    pallas_call x1, Pallas kernels, local(): pl.pallas_call(functools.partial(kernel, stages, L, T), out_shape=jax.Sha...  22.6 us
    unnamed x1, local copies, waits for them, and re-layouts  1.67 us

profile of v2, /device:TPU:0, one launch (start us, length us, event | category | flops | bytes accessed | tf_op | source)
XLA Modules:
  0.0 24.3 jit_solution(14364216436828374525)
XLA Ops:
  0.0 22.6 %shard_map.163 = bf16[8,8,8,256]{3,2,1,0:T(8,128)(2,1)} custom-call(bf16[8,8,8,256]{3,2,1,0:T(8,128)(2,1)} %refs_0_.1, f32[2,8,8]{2,1,0:T(8,128)} %refs_1_.1, s32[4,8,8]{2,1,0:T(8,128)} %refs_2_.1, bf16[256,1536]{1,0:T(8,128)(2,1)} %constant.2.clone.refs_3_, f32[256,256]{1,0:T(8,128)} %refs_4_.1, f32[64,256]{1,0:T(8,128)} %bitcast.2, f32[64,256]{1,0:T(8,128)} %refs_6_.1, ...), custom_call_target="tpu_custom_call" | custom-call | tf_op jit(solution)/shard_map/pallas_call | solution.py:431
  22.6 1.7 %copy.19 = bf16[8,8,8,256]{3,2,1,0:T(8,128)(2,1)} copy(bf16[8,8,8,256]{3,2,1,0:T(8,128)(2,1)} %shard_map.163) | data formatting | bytes 524288

commit v3 on v2

--- a/solution.py
+++ b/solution.py
@@ -12,7 +12,7 @@
 SQUARE = NODE * NODE
 F32 = jnp.float32
 BF16 = jnp.bfloat16
-VMEM_LIMIT = 60 * 1024 * 1024
+VMEM_LIMIT = 32 * 1024 * 1024
 MESH = pl.DeviceIdType.MESH
 
 
@@ -113,9 +113,9 @@
     (
         load_sem, force, near, w_second, level_one, down_one, solved, t0_ref, t1_ref,
         up_high, up_low, par_high, par_low,
-        send_x, send_y, halo_x, halo_y, halo_send, halo_recv,
-    ) = rest[len(names) : len(names) + 19]
-    stage_refs = rest[len(names) + 19 :]
+        send_x, send_y, halo_x, halo_y, halo_send, halo_recv, chain, fold_high, fold_low,
+    ) = rest[len(names) : len(names) + 22]
+    stage_refs = rest[len(names) + 22 :]
     T, L = tracer_count, leaf_side
     leaves = L * L
     rows = T * leaves
@@ -123,9 +123,9 @@
     loads = {}
     for k, name in enumerate(names):
         loads[name] = pltpu.make_async_copy(hbm[name], v[name], load_sem.at[k])
-    order = ["u", "tables", "velocity", "inflow", "leaf_skeleton"]
+    order = ["u", "tables", "velocity", "inflow", "parent_rest", "root_map", "leaf_skeleton"]
     order += ["merge_first", "merge_second", "merge_rest", "leaf_solve"]
-    order += ["sibling_first", "sibling_second", "sibling_rest", "parent_rest", "root_map"]
+    order += ["sibling_first", "sibling_second", "sibling_rest"]
     order += ["parent_second", "parent_first", "leaf_lift"]
     for name in order:
         loads[name].start()
@@ -176,6 +176,19 @@
         for c in range(2):
             line = pl.ds((2 + c) * rows + k * (L - 1), T * L, stride=L)
             send_y[k, c * T * L : (c + 1) * T * L, :] = near[line, :]
+    loads["parent_rest"].wait()
+    loads["root_map"].wait()
+    plan = [entry for stage in stages for entry in stage]
+    bits = [bit_of(axis, bit) for axis, bit in plan]
+    own_half = lambda k, w: jnp.where(bits[k] == 1, w[:, 128:], w[:, :128])
+    own_parent = lambda k: own_half(k, v["parent_rest"][4 + k])
+    previous = None
+    for k in range(len(plan)):
+        previous = own_parent(k) if k == 0 else product(own_parent(k), split(previous))
+        chain[k] = previous
+    chain[len(plan)] = product(v["root_map"][...], split(previous))
+    for k in range(4):
+        par_high[k], par_low[k] = split(v["parent_rest"][k])
     pl.semaphore_wait(barrier, expected)
 
     def halo_copy(axis, way):
@@ -344,18 +357,45 @@
             local_terms = [product(cats[k], split(v["sibling_rest"][k])) for k in range(4)]
             t1_ref[...] = product(cat_1, split(v["sibling_second"][...]))
             t0_ref[...] = product(cat_0, split(v["sibling_first"][...]))
-        if number == len(stages) - 1:
+        final = number == len(stages) - 1
+        if final:
+            first = len(plan) - len(stage)
+            weights = chain[len(plan)]
+            for k in reversed(range(first, len(plan))):
+                groups = weights.shape[1] // 128
+                weights = product(v["merge_rest"][4 + k], split(weights))
+                sibling = own_half(k, v["sibling_rest"][4 + k])
+                if k > 0:
+                    sibling = product(sibling, split(chain[k - 1]))
+                mine = jnp.int32(0)
+                for later in range(k + 1, len(plan)):
+                    mine = mine + bits[later] * (1 << (len(plan) - 1 - later))
+                blocks = [
+                    weights[:, g * 128 : (g + 1) * 128] + jnp.where(mine == g, sibling, 0.0)
+                    for g in range(groups)
+                ]
+                weights = jnp.concatenate(
+                    [x[:128] for x in blocks] + [x[128:] for x in blocks], axis=1
+                )
+            for g in range(slots):
+                fold_high[g], fold_low[g] = split(weights[:, g * 128 : (g + 1) * 128])
+            known = jnp.zeros((T, 128), F32)
+            for k, term in enumerate(path):
+                term = own_half(k, term)
+                known = known + (product(term, split(chain[k - 1])) if k > 0 else term)
             solved[...] = product(forcing, split(v["leaf_solve"][...]))
-            for name in ("parent_rest", "root_map", "parent_second", "parent_first", "leaf_lift"):
+            for name in ("parent_second", "parent_first", "leaf_lift"):
                 loads[name].wait()
-            for k in range(depth):
-                par_high[k], par_low[k] = split(v["parent_rest"][k])
-            w_root = split(v["root_map"][...])
             w_parent_second = split(v["parent_second"][...])
             w_parent_first = split(twice(v["parent_first"][...], 0))
             w_lift = split(twice(v["leaf_lift"][...], 0))
         for copy in copies:
             copy.wait()
+        if final:
+            slabs = jnp.concatenate([pool[g] for g in range(slots)], axis=1)
+            fold = [x[...].reshape(slots * 128, 128) for x in (fold_high, fold_low)]
+            boundary = product(slabs, fold) + known
+            break
         current = pool[...].reshape(slots * T, 128)
         for k, (axis, bit) in enumerate(stage):
             cat = joined(current)
@@ -363,15 +403,11 @@
             for later_axis, later_bit in stage[k + 1 :]:
                 middle = mine.shape[0] // 2
                 mine = jnp.where(bit_of(later_axis, later_bit) == 1, mine[middle:], mine[:middle])
-            path.append((level, bit_of(axis, bit), product(mine, split(v["sibling_rest"][level]))))
+            path.append(product(mine, split(v["sibling_rest"][level])))
             current = product(cat, up(level))
             level += 1
 
     down = lambda k: (par_high[k], par_low[k])
-    boundary = product(current, w_root)
-    for level, bit, term in reversed(path):
-        both = product(boundary, down(level)) + term
-        boundary = jnp.where(bit == 1, both[:, 128:], both[:, :128])
     for k in reversed(range(4)):
         both = product(boundary, down(k)) + local_terms[k]
         boundary = jnp.concatenate([both[:, :128], both[:, 128:]], axis=0)
@@ -416,14 +452,17 @@
         vmem((rows // 4, 128), F32),
         vmem((depth, 256, 128), BF16),
         vmem((depth, 256, 128), BF16),
-        vmem((depth, 128, 256), BF16),
-        vmem((depth, 128, 256), BF16),
+        vmem((4, 128, 256), BF16),
+        vmem((4, 128, 256), BF16),
         vmem((2, T * L, 128), F32),
         vmem((2, 2 * T * L, 128), F32),
         vmem((2, T * L, 128), F32),
         vmem((2, 2 * T * L, 128), F32),
         dma((4,)),
         dma((4,)),
+        vmem((depth, 128, 128), F32),
+        vmem((1 << len(stages[-1]), 128, 128), BF16),
+        vmem((1 << len(stages[-1]), 128, 128), BF16),
     ]
     for stage in stages:
         slots = 1 << len(stage)
@@ -437,7 +476,7 @@
         compiler_params=pltpu.CompilerParams(
             collective_id=0, has_side_effects=True, vmem_limit_bytes=VMEM_LIMIT
         ),
-    )(*args)
+    )(*[pltpu.with_memory_space_constraint(a, pltpu.HBM) for a in args])
 
 
 def solution(mesh):

time: 24.4 us -> 22.6 us (0.926)
  local copies, waits for them, and re-layouts: 1.67 us -> 0.71 us
  Pallas kernels: 22.6 us -> 21.7 us
    unnamed x1, local copies, waits for them, and re-layouts: 1.67 us -> 0.71 us
    pallas_call x1, Pallas kernels: 22.6 us -> 21.7 us  [local(): pl.pallas_call(functools.partial(kernel, stages, L, T), out_shape=jax.Sha...]
where the time goes in v3:
time: 22.6 us; the launch traced here: 22.4 us
  Pallas kernels  21.7 us (96%)
  local copies, waits for them, and re-layouts  0.71 us (3%)
    pallas_call x1, Pallas kernels, local(): pl.pallas_call(functools.partial(kernel, stages, L, T), out_shape=jax.Sha...  21.7 us
    unnamed x1, local copies, waits for them, and re-layouts  0.71 us

profile of v3, /device:TPU:0, one launch (start us, length us, event | category | flops | bytes accessed | tf_op | source)
XLA Modules:
  0.0 22.4 jit_solution(8437633013466238547)
XLA Ops:
  0.0 21.7 %shard_map.163 = bf16[8,8,8,256]{3,2,1,0:T(8,128)(2,1)S(1)} custom-call(bf16[8,8,8,256]{3,2,1,0:T(8,128)(2,1)} %refs_0_.1, f32[2,8,8]{2,1,0:T(8,128)} %refs_1_.1, s32[4,8,8]{2,1,0:T(8,128)} %refs_2_.1, bf16[256,1536]{1,0:T(8,128)(2,1)} %constant.2.clone.refs_3_, f32[256,256]{1,0:T(8,128)} %refs_4_.1, f32[64,256]{1,0:T(8,128)} %bitcast.2, f32[64,256]{1,0:T(8,128)} %refs_6_.1, ...), custom_call_target="tpu_custom_call" | custom-call | tf_op jit(solution)/shard_map/pallas_call | solution.py:470
  21.7 0.7 %copy.19 = bf16[8,8,8,256]{3,2,1,0:T(8,128)(2,1)} copy(bf16[8,8,8,256]{3,2,1,0:T(8,128)(2,1)S(1)} %shard_map.163) | data formatting | bytes 524288

commit v4 on v3

--- a/solution.py
+++ b/solution.py
@@ -123,9 +123,9 @@
     loads = {}
     for k, name in enumerate(names):
         loads[name] = pltpu.make_async_copy(hbm[name], v[name], load_sem.at[k])
-    order = ["u", "tables", "velocity", "inflow", "parent_rest", "root_map", "leaf_skeleton"]
+    order = ["u", "tables", "velocity", "inflow", "leaf_skeleton"]
     order += ["merge_first", "merge_second", "merge_rest", "leaf_solve"]
-    order += ["sibling_first", "sibling_second", "sibling_rest"]
+    order += ["sibling_first", "sibling_second", "sibling_rest", "parent_rest", "root_map"]
     order += ["parent_second", "parent_first", "leaf_lift"]
     for name in order:
         loads[name].start()
@@ -168,27 +168,20 @@
     facing = dot(ub, v["tables"][:, 4 * SQUARE :])
     for c in range(4):
         near[c * rows : (c + 1) * rows, :] = facing[:, c * 128 : (c + 1) * 128]
-    for t in range(T):
-        base = t * leaves
-        send_x[1, t * L : (t + 1) * L, :] = facing[base + leaves - L : base + leaves, :128]
-        send_x[0, t * L : (t + 1) * L, :] = facing[base : base + L, 128:256]
+    lines = lambda start, c: jnp.concatenate(
+        [
+            facing[t * leaves + start : t * leaves + start + L, c * 128 : (c + 1) * 128]
+            for t in range(T)
+        ],
+        axis=0,
+    )
+    send_x[1] = lines(leaves - L, 0).astype(BF16)
+    send_x[0] = lines(0, 1).astype(BF16)
     for k in range(2):
-        for c in range(2):
-            line = pl.ds((2 + c) * rows + k * (L - 1), T * L, stride=L)
-            send_y[k, c * T * L : (c + 1) * T * L, :] = near[line, :]
-    loads["parent_rest"].wait()
-    loads["root_map"].wait()
-    plan = [entry for stage in stages for entry in stage]
-    bits = [bit_of(axis, bit) for axis, bit in plan]
-    own_half = lambda k, w: jnp.where(bits[k] == 1, w[:, 128:], w[:, :128])
-    own_parent = lambda k: own_half(k, v["parent_rest"][4 + k])
-    previous = None
-    for k in range(len(plan)):
-        previous = own_parent(k) if k == 0 else product(own_parent(k), split(previous))
-        chain[k] = previous
-    chain[len(plan)] = product(v["root_map"][...], split(previous))
-    for k in range(4):
-        par_high[k], par_low[k] = split(v["parent_rest"][k])
+        parts = [
+            near[pl.ds((2 + c) * rows + k * (L - 1), T * L, stride=L), :] for c in range(2)
+        ]
+        send_y[k] = (parts[0] + pltpu.roll(parts[1], 2, 1)).astype(BF16)
     pl.semaphore_wait(barrier, expected)
 
     def halo_copy(axis, way):
@@ -281,7 +274,7 @@
             k = 0 if way < 0 else 1
             halo_copy(axis, way).wait_send()
             halo_copy(axis, -way).wait_recv()
-            arrived = (halo_x if axis == "gx" else halo_y)[1 - k]
+            arrived = (halo_x if axis == "gx" else halo_y)[1 - k].astype(F32)
             if axis == "gx":
                 edge = 0 if way < 0 else leaves - L
                 weight = weight_0[:L] if way < 0 else weight_1[leaves - L :]
@@ -295,7 +288,7 @@
                     weight = w_second[pl.ds((2 * k + c) * leaves + edge, L, stride=L), :]
                     weight = jnp.concatenate([weight] * T, axis=0)
                     at = pl.ds(c * rows + edge, T * L, stride=L)
-                    line = arrived[c * T * L : (c + 1) * T * L]
+                    line = arrived if c == 0 else pltpu.roll(arrived, 126, 1)
                     force[at, :] = force[at, :] + weight * line
 
     forcing = jnp.concatenate([force[:rows, :], force[rows:, :]], axis=1)
@@ -330,6 +323,10 @@
         current = product(cats[-1], up(k))
 
     level = 4
+    plan = [entry for stage in stages for entry in stage]
+    bits = [bit_of(axis, bit) for axis, bit in plan]
+    own_half = lambda k, w: jnp.where(bits[k] == 1, w[:, 128:], w[:, :128])
+    own_parent = lambda k: own_half(k, v["parent_rest"][4 + k])
     path = []
     for number, stage in enumerate(stages):
         pool, stage_send, stage_recv = stage_refs[3 * number : 3 * number + 3]
@@ -357,6 +354,15 @@
             local_terms = [product(cats[k], split(v["sibling_rest"][k])) for k in range(4)]
             t1_ref[...] = product(cat_1, split(v["sibling_second"][...]))
             t0_ref[...] = product(cat_0, split(v["sibling_first"][...]))
+            loads["parent_rest"].wait()
+            loads["root_map"].wait()
+            previous = None
+            for k in range(len(plan)):
+                previous = own_parent(k) if k == 0 else product(own_parent(k), split(previous))
+                chain[k] = previous
+            chain[len(plan)] = product(v["root_map"][...], split(previous))
+            for k in range(4):
+                par_high[k], par_low[k] = split(v["parent_rest"][k])
         final = number == len(stages) - 1
         if final:
             first = len(plan) - len(stage)
@@ -454,10 +460,10 @@
         vmem((depth, 256, 128), BF16),
         vmem((4, 128, 256), BF16),
         vmem((4, 128, 256), BF16),
-        vmem((2, T * L, 128), F32),
-        vmem((2, 2 * T * L, 128), F32),
-        vmem((2, T * L, 128), F32),
-        vmem((2, 2 * T * L, 128), F32),
+        vmem((2, T * L, 128), BF16),
+        vmem((2, T * L, 128), BF16),
+        vmem((2, T * L, 128), BF16),
+        vmem((2, T * L, 128), BF16),
         dma((4,)),
         dma((4,)),
         vmem((depth, 128, 128), F32),

time: 22.6 us -> 20.1 us (0.89)
  Pallas kernels: 21.7 us -> 19.3 us
    pallas_call x1, Pallas kernels: 21.7 us -> 19.3 us  [local(): pl.pallas_call(functools.partial(kernel, stages, L, T), out_shape=jax.Sha...]
where the time goes in v4:
time: 20.1 us; the launch traced here: 20 us
  Pallas kernels  19.3 us (96%)
  local copies, waits for them, and re-layouts  0.71 us (4%)
    pallas_call x1, Pallas kernels, local(): pl.pallas_call(functools.partial(kernel, stages, L, T), out_shape=jax.Sha...  19.3 us
    unnamed x1, local copies, waits for them, and re-layouts  0.71 us

profile of v4, /device:TPU:0, one launch (start us, length us, event | category | flops | bytes accessed | tf_op | source)
XLA Modules:
  0.0 20.0 jit_solution(12309669341698849820)
XLA Ops:
  0.0 19.3 %shard_map.163 = bf16[8,8,8,256]{3,2,1,0:T(8,128)(2,1)S(1)} custom-call(bf16[8,8,8,256]{3,2,1,0:T(8,128)(2,1)} %refs_0_.1, f32[2,8,8]{2,1,0:T(8,128)} %refs_1_.1, s32[4,8,8]{2,1,0:T(8,128)} %refs_2_.1, bf16[256,1536]{1,0:T(8,128)(2,1)} %constant.2.clone.refs_3_, f32[256,256]{1,0:T(8,128)} %refs_4_.1, f32[64,256]{1,0:T(8,128)} %bitcast.2, f32[64,256]{1,0:T(8,128)} %refs_6_.1, ...), custom_call_target="tpu_custom_call" | custom-call | tf_op jit(solution)/shard_map/pallas_call | solution.py:476
  19.3 0.7 %copy.19 = bf16[8,8,8,256]{3,2,1,0:T(8,128)(2,1)} copy(bf16[8,8,8,256]{3,2,1,0:T(8,128)(2,1)S(1)} %shard_map.163) | data formatting | bytes 524288
